TPU v7x, 256 devices: a whole 4x4x8 slice. The times are simulated.
256 devices in a mesh: branch: 8 (over x, core), col: 32 (over z, y).
Axes of the slice: x: 4, y: 4, z: 8, core: 2. Of those that a mesh axis runs over, the one named last changes fastest.
Arguments:
- child_fronts: float32 [8, 4096, 4096], P('branch', None, 'col'), as said below
- extend_map: int32 [8, 14], P('branch'), may hold values from 0 to 15, as said below
- parent_front: float32 [4096, 4096], P('branch', 'col'), as said below
Outputs:
- child_factor: float32 [8, 512, 4096], P('branch', None, 'col')
- parent_factor: float32 [512, 4096], P(None, 'col')
- parent_update: float32 [4096, 4096], P('branch', 'col')
Inputs may be any that keep to these rules, and one draw needn't show every extreme that they name: Each row of extend_map names 14 different parent blocks; some row names block 0 and some row names block 15. `child_fronts`: each child front is symmetric and positive definite. `parent_front`: the parent front is symmetric and positive definite.
All inputs are finite; a program needn't handle non-finite values.
Results may differ from a plain program's by a relative error of at most 0.0003.
Values sent between devices are 32-bit elements; how exact they have to be, the bound alone decides.
A program may use at most 128 MiB of HBM per device.

v0:
```python
import jax
import jax.numpy as jnp
from jax import lax
from jax.experimental import pallas as pl
from jax.experimental.pallas import tpu as pltpu
from jax.sharding import PartitionSpec as P

BS = 256
P_SIZE = 512
NP = 4096
PP = 512
HB = 128
NZ, NY = 8, 4
NH = NZ * NY
LO = 32
F32 = jnp.float32
HI = lax.Precision.HIGHEST
VMEM = pl.BlockSpec(memory_space=pltpu.VMEM)
SMEM = pl.BlockSpec(memory_space=pltpu.SMEM)
ANY = pl.BlockSpec(memory_space=pl.ANY)


def dot(a, b, dims):
    return lax.dot_general(a, b, (dims, ((), ())), precision=HI, preferred_element_type=F32)


def lane(x, i):
    return jnp.broadcast_to(x[:, i : i + 1], (8, 128))


def sub(x, i):
    return jnp.broadcast_to(x[i : i + 1, :], (8, x.shape[1]))


def chol_inv_128(tiles, hook=None):
    row = lax.broadcasted_iota(jnp.int32, (8, 128), 0)
    col = lax.broadcasted_iota(jnp.int32, (8, 128), 1)
    D = list(tiles)
    E = [jnp.where(col == row + 8 * q, 1.0, 0.0).astype(F32) for q in range(16)]
    for p in range(16):
        if hook is not None:
            hook(p)
        a, e = D[p], E[p]
        C = [lane(a, 8 * p + k) for k in range(8)]
        for k in range(8):
            rs = lax.rsqrt(sub(C[k], k))
            l = C[k] * rs
            lm = jnp.where(row > k, l, 0.0)
            for j in range(k + 1, 8):
                C[j] = C[j] - l * sub(l, j)
            ra = sub(a, k) * rs
            re = sub(e, k) * rs
            a = jnp.where(row == k, ra, a - lm * ra)
            e = jnp.where(row == k, re, e - lm * re)
        E[p] = e
        if p < 15:
            at = a.T
            for q in range(p + 1, 16):
                t, u = D[q], E[q]
                for k in range(8):
                    m = jnp.broadcast_to(at[8 * q : 8 * q + 8, k : k + 1], (8, 128))
                    t = t - m * sub(a, k)
                    u = u - m * sub(e, k)
                D[q], E[q] = t, u
    return E


def chol_inverse(rows, s_ref, m_ref, hooks=None):
    m_ref[...] = jnp.zeros((512, 512), F32)
    for b in range(4):
        o = 128 * b
        blk = slice(o, o + 128)
        A = rows(b)
        if b:
            A = A - dot(s_ref[:o, blk], s_ref[:o, o:], ((0,), (0,)))
        tiles = [A[8 * q : 8 * q + 8, :128] for q in range(16)]
        s_ref[blk, o:] = A
        W = jnp.concatenate(chol_inv_128(tiles, None if hooks is None else hooks(b)), axis=0)
        m_ref[blk, blk] = W
        if b < 3:
            s_ref[blk, o + 128 :] = dot(W, s_ref[blk, o + 128 :], ((1,), (0,)))
        if b:
            m_ref[blk, :o] = -dot(W, dot(s_ref[:o, blk], m_ref[:o, :o], ((0,), (0,))), ((1,), (0,)))


def chol_inverse_loop(rows, s_ref, m_ref, hook):
    m_ref[...] = jnp.zeros((512, 512), F32)
    s_ref[...] = jnp.zeros((512, 512), F32)

    @pl.loop(0, 4)
    def _(b):
        hook(b)
        o = pl.multiple_of(128 * b, 128)
        blk = pl.ds(o, 128)
        lead = s_ref[:, blk]
        A = rows(b) - dot(lead, s_ref[...], ((0,), (0,)))
        s_ref[blk, :] = A
        tiles = [s_ref[pl.ds(o + 8 * q, 8), blk] for q in range(16)]
        W = jnp.concatenate(chol_inv_128(tiles), axis=0)
        m_ref[blk, :] = -dot(W, dot(lead, m_ref[...], ((0,), (0,))), ((1,), (0,)))
        m_ref[blk, blk] = W
        s_ref[blk, :] = dot(W, A, ((1,), (0,)))


def child_kernel(
    map_ref, front_hbm, g_ref, t_ref,
    front_ref, tt_ref, send_ref, all_ref, recv_ref, s_ref, m_ref, p_ref, tab_ref,
    s0y, r0y, s0z, r0z, s1z, r1z, s1y, r1y, s1f, r1f, sf, rf, loc,
):
    me = lax.axis_index("col")
    core = lax.rem(lax.axis_index("branch"), 2)
    z, y = me // NY, lax.rem(me, NY)
    d = 1 - 2 * core

    top = pltpu.make_async_copy(
        front_hbm.at[pl.ds(0, 4)], front_ref.at[pl.ds(0, 4)], loc.at[0]
    )
    top.start()
    rest = pltpu.make_async_copy(
        front_hbm.at[pl.ds(4, NH - 4)], front_ref.at[pl.ds(4, NH - 4)], loc.at[1]
    )
    rest.start()

    def at(zz, yy):
        return lax.rem(zz + 2 * NZ, NZ) * NY + lax.rem(yy + NY, NY)

    barrier = pltpu.get_barrier_semaphore()

    @pl.loop(1, NH)
    def _(k):
        pl.semaphore_signal(barrier, inc=1, device_id={"col": lax.rem(me + k, NH)})

    for b in range(NP // BS):
        at_u = jnp.int32(-1)
        for u in range(14):
            at_u = jnp.where(map_ref[0, u] == b, u, at_u)
        keep = (at_u >= 0).astype(jnp.int32)
        src = jnp.where(at_u >= 0, 2 * at_u + 4, 0)
        for part in range(2):
            tab_ref[0, 2 * b + part] = src + part
            tab_ref[1, 2 * b + part] = keep

    top.wait()
    for k in range(4):
        tt_ref[:, 128 * k : 128 * k + 128] = front_ref[k].T

    pl.semaphore_wait(barrier, NH - 1)

    def copy(src, dst, ss, rs, to):
        return pltpu.make_async_remote_copy(
            src_ref=src, dst_ref=dst, send_sem=ss, recv_sem=rs, device_id={"col": to}
        )

    lo, hi = pl.ds(0, LO), pl.ds(LO, HB - LO)
    mid = (HB - LO) // 2
    half = (pl.ds(LO, mid), pl.ds(LO + mid, mid))
    own = pltpu.make_async_copy(tt_ref, all_ref.at[me], loc.at[2])
    own.start()

    order = [0, 1, -1, 2, -2, 3, -3, 4]
    fwd, bwd = [0, 1, 3, 5, 7], [0, 2, 4, 6]

    def behind(i):
        if isinstance(i, int):
            return order[i]
        return ((i + 1) // 2) * (2 * lax.rem(i, 2) - 1)

    def z1_send(chain, n, src=None):
        i, slot = chain[n], chain[n + 1]
        step = d if chain is fwd else -d
        blk = at(z - order[i] * d, y)
        src = all_ref.at[blk, hi] if src is None else src
        return copy(src, all_ref.at[blk, hi], s1z.at[slot - 1], r1z.at[slot - 1], at(z + step, y))

    def z1_recv(slot):
        ref = all_ref.at[at(z - order[slot] * d, y), hi]
        return copy(ref, ref, s1z.at[slot - 1], r1z.at[slot - 1], me)

    def y1(i, side, src=None):
        blk = at(z - behind(i) * d, y)
        src = all_ref.at[blk, hi] if src is None else src
        return copy(src, all_ref.at[blk, hi], s1y.at[i, side], r1y.at[i, side], at(z, y + 1 - 2 * side))

    def y1_recv(i, side):
        ref = all_ref.at[at(z - behind(i) * d, y - 1 + 2 * side), hi]
        return copy(ref, ref, s1y.at[i, side], r1y.at[i, side], me)

    def y1f(i, side):
        ref = all_ref.at[at(z - behind(i) * d, y - 1 + 2 * side), half[side]]
        return copy(ref, ref, s1f.at[i, side], r1f.at[i, side], at(z, y + 1 - 2 * side))

    def y1f_recv(i, side):
        ref = all_ref.at[at(z - behind(i) * d, y + 2), half[side]]
        return copy(ref, ref, s1f.at[i, side], r1f.at[i, side], me)

    def y0(k, src):
        return copy(src, all_ref.at[me, lo], s0y.at[k - 1], r0y.at[k - 1], at(z, y + k))

    def y0_recv(k):
        ref = all_ref.at[at(z, y - k), lo]
        return copy(ref, ref, s0y.at[k - 1], r0y.at[k - 1], me)

    def bundle(i):
        return all_ref.at[pl.ds(at(z - order[i] * d, 0), NY), lo]

    def z0_send(chain, n):
        i, slot = chain[n], chain[n + 1]
        step = d if chain is fwd else -d
        return copy(bundle(i), bundle(i), s0z.at[slot - 1], r0z.at[slot - 1], at(z + step, y))

    def z0_recv(slot):
        return copy(bundle(slot), bundle(slot), s0z.at[slot - 1], r0z.at[slot - 1], me)

    def fsend(k):
        to = lax.rem(me + k, NH)
        return copy(send_ref.at[to], recv_ref.at[me], sf.at[k - 1], rf.at[k - 1], to)

    def frecv(k):
        frm = lax.rem(me + NH - k, NH)
        return copy(send_ref.at[frm], recv_ref.at[frm], sf.at[k - 1], rf.at[k - 1], frm)

    def picked(h):
        return front_ref[tab_ref[0, h]].T * tab_ref[1, h].astype(F32)

    def prepare(first, last):
        @pl.loop(first, last)
        def _(k):
            h = lax.rem(me + k, NH)
            send_ref[h] = picked(h)

    def start_f(first, last):
        @pl.loop(first, last)
        def _(k):
            fsend(k).start()

    sends = []

    def go(c):
        c.start()
        sends.append(c)

    go(z1_send(fwd, 0, tt_ref.at[hi]))
    go(z1_send(bwd, 0, tt_ref.at[hi]))
    for k in (1, 3, 2):
        go(y0(k, tt_ref.at[lo]))
    for side in (0, 1):
        go(y1(0, side, tt_ref.at[hi]))
    rest.wait()
    prepare(1, 12)
    own.wait()
    for k in (1, 3, 2):
        y0_recv(k).wait_recv()
    go(z0_send(fwd, 0))
    go(z0_send(bwd, 0))
    for n in range(1, 5):
        for chain in (fwd, bwd):
            if n < len(chain):
                slot = chain[n]
                z1_recv(slot).wait_recv()
                if n + 1 < len(chain):
                    go(z1_send(chain, n))
                for side in (0, 1):
                    go(y1(slot, side))
        if n == 1:
            prepare(12, NH)
            recv_ref[me] = picked(me)
        for chain in (fwd, bwd):
            if n < len(chain):
                z0_recv(chain[n]).wait_recv()
                if n + 1 < len(chain):
                    go(z0_send(chain, n))
        start_f(1 + 4 * (n - 1), 1 + 4 * n)

    dist = lax.rem(z * d + NZ, NZ)
    i0 = jnp.where(dist <= 4, jnp.where(dist == 0, 0, 2 * dist - 1), 2 * (NZ - dist))
    for side in (0, 1):
        y1_recv(i0, side).wait_recv()
        y1f(i0, side).start()
    start_f(17, NH)
    for side in (0, 1):
        y1f_recv(i0, side).wait_recv()

    def forward(b):
        for n in range(2):
            i = 2 * b + n

            @pl.when(i != i0)
            def _():
                for side in (0, 1):
                    y1_recv(i, side).wait_recv()
                    y1f(i, side).start()

    chol_inverse_loop(lambda b: all_ref[b], s_ref, m_ref, forward)
    M = m_ref[...]
    g_ref[...] = dot(M, all_ref[me], ((1,), (1,)))

    @pl.loop(0, 8)
    def _(i):
        @pl.when(i != i0)
        def _():
            for side in (0, 1):
                y1f_recv(i, side).wait_recv()

    Y = dot(M, all_ref[tab_ref[0, me]], ((1,), (1,)))
    s_ref[:, :HB] = dot(M, Y, ((0,), (0,)))

    @pl.loop(0, NH // 4)
    def _(i):
        rows = all_ref[pl.ds(4 * i, 4)].reshape(4 * HB, P_SIZE)
        p_ref[pl.ds(4 * i, 4)] = dot(rows, s_ref[:, :HB], ((1,), (0,))).reshape(4, HB, HB)

    @pl.loop(1, NH)
    def _(k):
        frecv(k).wait_recv()

    keep_me = tab_ref[1, me].astype(F32)

    @pl.loop(0, NH)
    def _(p):
        q = tab_ref[0, p]
        keep = tab_ref[1, p].astype(F32)
        t_ref[p] = keep * (recv_ref[q] - keep_me * p_ref[q])

    for c in sends:
        c.wait_send()

    @pl.loop(0, 8)
    def _(i):
        for side in (0, 1):
            y1f(i, side).wait_send()

    @pl.loop(1, NH)
    def _(k):
        fsend(k).wait_send()


def child(extend_map, front):
    dma = pltpu.SemaphoreType.DMA
    return pl.pallas_call(
        child_kernel,
        out_shape=(
            jax.ShapeDtypeStruct((P_SIZE, HB), F32),
            jax.ShapeDtypeStruct((NH, HB, HB), F32),
        ),
        in_specs=[SMEM, ANY],
        out_specs=(VMEM, VMEM),
        scratch_shapes=[
            pltpu.VMEM((NH, HB, HB), F32),
            pltpu.VMEM((HB, P_SIZE), F32),
            pltpu.VMEM((NH, HB, HB), F32),
            pltpu.VMEM((NH, HB, P_SIZE), F32),
            pltpu.VMEM((NH, HB, HB), F32),
            pltpu.VMEM((P_SIZE, P_SIZE), F32),
            pltpu.VMEM((P_SIZE, P_SIZE), F32),
            pltpu.VMEM((NH, HB, HB), F32),
            pltpu.SMEM((2, NH), jnp.int32),
            dma((3,)), dma((3,)), dma((7,)), dma((7,)), dma((7,)), dma((7,)),
            dma((8, 2)), dma((8, 2)), dma((8, 2)), dma((8, 2)),
            dma((31,)), dma((31,)), dma((3,)),
        ],
        compiler_params=pltpu.CompilerParams(
            collective_id=0, has_side_effects=True, vmem_limit_bytes=48 << 20
        ),
        name="child",
    )(extend_map, front)


PANEL = {(0, 1): 0, (0, 10): 1, (1, 7): 2, (2, 4): 3, (3, 1): 4}


def parent_kernel(
    t_ref, pf_ref, fac_ref, out_ref,
    rtop, part, top, piv, pan, rx, sx, r2, s_ref, m_ref,
    s_rs, r_rs, s_pf, r_pf, s_ag, r_ag, s_x, r_x, s_2, r_2,
    s_vz, r_vz, s_vy, r_vy, s_nz, r_nz, s_ny, r_ny, loc,
):
    br, me = lax.axis_index("branch"), lax.axis_index("col")
    x, core = br // 2, lax.rem(br, 2)
    z, y = me // NY, lax.rem(me, NY)
    nb = 8

    def along_z(k):
        return lax.rem(z + k, NZ) * NY + y

    def along_y(k):
        return z * NY + lax.rem(y + k, NY)

    barrier = pltpu.get_barrier_semaphore()
    for k in range(1, nb):
        pl.semaphore_signal(barrier, inc=1, device_id={"branch": lax.rem(br + k, nb)})
    for k in range(1, NZ):
        pl.semaphore_signal(barrier, inc=1, device_id={"col": along_z(k)})
    for k in range(1, NY):
        pl.semaphore_signal(barrier, inc=1, device_id={"col": along_y(k)})
    pl.semaphore_wait(barrier, nb - 1 + NZ - 1 + NY - 1)

    def copy(src, dst, ss, rs, **to):
        return pltpu.make_async_remote_copy(
            src_ref=src, dst_ref=dst, send_sem=ss, recv_sem=rs, device_id=to
        )

    def piece(b):
        return pl.ds(pl.multiple_of(16 * b, 16), 16)

    def rs_send(k):
        to = lax.rem(br + k, nb)
        return copy(t_ref.at[pl.ds(0, 4), piece(to)], rtop.at[br], s_rs.at[k - 1], r_rs.at[k - 1], branch=to)

    def rs_recv(k):
        frm = lax.rem(br + nb - k, nb)
        return copy(rtop.at[frm], rtop.at[frm], s_rs.at[k - 1], r_rs.at[k - 1], branch=frm)

    def pf_send(k):
        return copy(pf_ref.at[:, piece(k)], rtop.at[nb], s_pf.at[k - 1], r_pf, branch=jnp.int32(k))

    for k in range(1, nb):
        rs_send(k).start()

    @pl.when(br == 0)
    def _():
        for k in range(1, nb):
            pf_send(k).start()

    def x_send(i):
        grp = 2 * i + 1 - core
        return copy(t_ref.at[pl.ds(4 * grp, 4)], rx.at[i], s_x.at[i], r_x.at[i], branch=br + 1 - 2 * core)

    for i in range(4):
        x_send(i).start()

    own = t_ref[0:4, piece(br), :]
    for k in range(1, nb):
        rs_recv(k).wait_recv()
        own = own + rtop[lax.rem(br + nb - k, nb)]
    part[...] = own

    @pl.when(br == 0)
    def _():
        part[...] += pf_ref[:, 0:16, :]

    @pl.when(br != 0)
    def _():
        copy(rtop.at[nb], rtop.at[nb], s_pf.at[0], r_pf, branch=jnp.int32(0)).wait_recv()
        part[...] += rtop[nb]

    def ag_send(k):
        to = lax.rem(br + k, nb)
        return copy(part, top.at[:, piece(br)], s_ag.at[k - 1], r_ag.at[k - 1], branch=to)

    def ag_recv(k):
        ref = top.at[:, piece(lax.rem(br + nb - k, nb))]
        return copy(part, ref, s_ag.at[k - 1], r_ag.at[k - 1], branch=br)

    for k in range(1, nb):
        ag_send(k).start()
    top[:, piece(br), :] = part[...]
    for k in range(1, nb):
        ag_recv(k).wait_recv()

    def chain(dist):
        step = jnp.where(dist <= 4, 1, NZ - 1)
        return step, jnp.logical_and(dist != 0, jnp.logical_and(dist != 4, dist != 5))

    vstep, vmore = chain(z)
    ndist = lax.rem(z + NZ - br, NZ)
    nstep, nmore = chain(ndist)
    nhops = jnp.minimum(ndist, NZ - ndist)

    def vy(b, k):
        return copy(piv.at[y, b], piv.at[y, b], s_vy.at[b, k - 1], r_vy.at[b, k - 1], col=along_y(k))

    def vy_recv(b, k):
        ref = piv.at[lax.rem(y + NY - k, NY), b]
        return copy(ref, ref, s_vy.at[b, k - 1], r_vy.at[b, k - 1], col=me)

    def ny(k):
        return copy(pan.at[y], pan.at[y], s_ny.at[k - 1], r_ny.at[k - 1], col=along_y(k))

    def ny_recv(k):
        ref = pan.at[lax.rem(y + NY - k, NY)]
        return copy(ref, ref, s_ny.at[k - 1], r_ny.at[k - 1], col=me)

    lpiv = pltpu.make_async_copy(top, piv.at[y], loc.at[0])
    lpan = pltpu.make_async_copy(top, pan.at[y], loc.at[1])

    @pl.when(z == 0)
    def _():
        lpiv.start()
        for b in range(4):
            copy(top.at[b], piv.at[y, b], s_vz.at[b, 0], r_vz.at[b], col=along_z(1)).start()
            copy(top.at[b], piv.at[y, b], s_vz.at[b, 1], r_vz.at[b], col=along_z(7)).start()
        lpiv.wait()

    @pl.when(z == br)
    def _():
        lpan.start()
        copy(top, pan.at[y], s_nz.at[0], r_nz, col=along_z(1)).start()
        copy(top, pan.at[y], s_nz.at[1], r_nz, col=along_z(7)).start()
        lpan.wait()

    def spread(b):
        @pl.when(z != 0)
        def _():
            copy(piv.at[y, b], piv.at[y, b], s_vz.at[b, 0], r_vz.at[b], col=me).wait_recv()

        @pl.when(vmore)
        def _():
            copy(piv.at[y, b], piv.at[y, b], s_vz.at[b, 0], r_vz.at[b], col=along_z(vstep)).start()

        for k in (2, 1, 3):
            vy(b, k).start()

    def panel_step(hops):
        @pl.when(nhops == hops)
        def _():
            if hops:
                copy(top, pan.at[y], s_nz.at[0], r_nz, col=me).wait_recv()

            @pl.when(nmore)
            def _():
                copy(pan.at[y], pan.at[y], s_nz.at[0], r_nz, col=along_z(nstep)).start()

            for k in (2, 1, 3):
                ny(k).start()

    def rows(b):
        for k in (1, 3, 2):
            vy_recv(b, k).wait_recv()
        return jnp.concatenate([piv[j, b] for j in range(b, 4)], axis=1)

    def x_recv(i):
        return copy(rx.at[i], rx.at[i], s_x.at[i], r_x.at[i], branch=br)

    def send2(k):
        to = lax.rem(x + k, 4)
        return copy(sx.at[to], r2.at[k - 1], s_2.at[k - 1], r_2.at[k - 1], branch=2 * to + core)

    def hooks(b):
        def hook(p):
            if p == 12 and b < 3:
                spread(b + 1)
            if b == 0 and p == 6:
                for i in range(4):
                    x_recv(i).wait_recv()

                @pl.loop(0, 4)
                def _(i):
                    sx[i] = rx[i] + t_ref[pl.ds(4 * (2 * i + core), 4)]

            if b == 0 and p == 9:
                for k in (2, 1, 3):
                    send2(k).start()
            if (b, p) in PANEL:
                panel_step(PANEL[b, p])

        return hook

    spread(0)
    chol_inverse(rows, s_ref, m_ref, hooks)
    M = m_ref[...]
    F = dot(M, top[...].reshape(PP, HB), ((1,), (0,)))
    fac_ref[...] = F
    Z = dot(M, F, ((0,), (0,)))
    for k in range(1, 4):
        send2(k).wait_recv()
    for k in (1, 3, 2):
        ny_recv(k).wait_recv()

    s_ref[:, :HB] = Z

    @pl.loop(0, 4)
    def _(j):
        asm = pf_ref[j] + sx[x, j] + r2[0, j] + r2[1, j] + r2[2, j]
        rowsj = pan[j].reshape(PP, HB)
        out_ref[j] = asm - dot(rowsj, s_ref[:, :HB], ((0,), (0,)))

    for k in range(1, nb):
        rs_send(k).wait_send()
        ag_send(k).wait_send()

    @pl.when(br == 0)
    def _():
        for k in range(1, nb):
            pf_send(k).wait_send()

    for i in range(4):
        x_send(i).wait_send()
    for k in range(1, 4):
        send2(k).wait_send()
        ny(k).wait_send()
        for b in range(4):
            vy(b, k).wait_send()

    for b in range(4):
        @pl.when(jnp.logical_or(z == 0, vmore))
        def _():
            copy(top.at[b], piv.at[y, b], s_vz.at[b, 0], r_vz.at[b], col=along_z(vstep)).wait_send()

        @pl.when(z == 0)
        def _():
            copy(top.at[b], piv.at[y, b], s_vz.at[b, 1], r_vz.at[b], col=along_z(7)).wait_send()

    @pl.when(jnp.logical_or(ndist == 0, nmore))
    def _():
        copy(top, pan.at[y], s_nz.at[0], r_nz, col=along_z(nstep)).wait_send()

    @pl.when(ndist == 0)
    def _():
        copy(top, pan.at[y], s_nz.at[1], r_nz, col=along_z(7)).wait_send()


def parent(strip, front):
    dma = pltpu.SemaphoreType.DMA
    return pl.pallas_call(
        parent_kernel,
        out_shape=(
            jax.ShapeDtypeStruct((PP, HB), F32),
            jax.ShapeDtypeStruct((4, HB, HB), F32),
        ),
        in_specs=[VMEM, VMEM],
        out_specs=(VMEM, VMEM),
        scratch_shapes=[
            pltpu.VMEM((9, 4, 16, HB), F32),
            pltpu.VMEM((4, 16, HB), F32),
            pltpu.VMEM((4, HB, HB), F32),
            pltpu.VMEM((4, 4, HB, HB), F32),
            pltpu.VMEM((4, 4, HB, HB), F32),
            pltpu.VMEM((4, 4, HB, HB), F32),
            pltpu.VMEM((4, 4, HB, HB), F32),
            pltpu.VMEM((3, 4, HB, HB), F32),
            pltpu.VMEM((PP, PP), F32),
            pltpu.VMEM((PP, PP), F32),
            dma((7,)), dma((7,)), dma((7,)), dma(()), dma((7,)), dma((7,)),
            dma((4,)), dma((4,)), dma((3,)), dma((3,)),
            dma((4, 2)), dma((4,)), dma((4, 3)), dma((4, 3)),
            dma((2,)), dma(()), dma((3,)), dma((3,)), dma((2,)),
        ],
        compiler_params=pltpu.CompilerParams(
            collective_id=1, has_side_effects=True, vmem_limit_bytes=48 << 20
        ),
        name="parent",
    )(strip, front)


def on_device(child_fronts, extend_map, parent_front):
    front = child_fronts[0]
    child_mine, strip = child(extend_map, front.reshape(NH, HB, HB))
    parent_mine, result = parent(strip, parent_front.reshape(4, HB, HB))
    return (child_mine[None], parent_mine, result.reshape(parent_front.shape))


def solution(mesh):
    in_specs = (P("branch", None, "col"), P("branch", None), P("branch", "col"))
    out_specs = (P("branch", None, "col"), P(None, "col"), P("branch", "col"))
    return jax.shard_map(
        on_device, mesh=mesh, in_specs=in_specs, out_specs=out_specs, check_vma=False
    )
```

profile of v0, /device:TPU:160, one launch (start us, length us, event | category | flops | bytes accessed | tf_op | source)
XLA Modules:
  0.0 218.2 jit_solution(4373438386197535318)
XLA Ops:
  0.6 0.0 copy-start
  0.6 1.6 copy-done
  2.2 0.0 copy-start.2
  2.2 0.7 copy-done.2
  2.9 0.0 copy-start.1
  2.9 123.3 %child.1 = (f32[512,128]{1,0:T(8,128)S(1)}, f32[32,128,128]{2,1,0:T(8,128)S(1)}) custom-call(s32[1,14]{1,0:T(1,128)S(1)} %copy-done.2, f32[32,128,128]{2,1,0:T(8,128)S(1)} %bitcast.4), custom_call_target="tpu_custom_call" | custom-call | tf_op jit(solution)/shard_map/child/pallas_call | solution.py:339
  126.2 0.0 copy-done.1
  126.2 89.9 %parent.1 = (f32[512,128]{1,0:T(8,128)S(1)}, f32[4,128,128]{2,1,0:T(8,128)S(1)}) custom-call(f32[32,128,128]{2,1,0:T(8,128)S(1)} %get-tuple-element.8.t_ref, f32[4,128,128]{2,1,0:T(8,128)S(1)} %bitcast.5), custom_call_target="tpu_custom_call" | custom-call | tf_op jit(solution)/shard_map/parent/pallas_call | solution.py:614
  216.1 0.7 copy.9
  216.8 0.7 copy.10
  217.5 0.7 copy.11
Async XLA Ops:
  0.6 1.6 copy-start
  2.2 0.7 copy-start.2
  2.9 123.3 %copy-start.1 = (f32[512,128]{1,0:T(8,128)S(1)}, f32[512,128]{1,0:T(8,128)}, u32[]{:S(2)}) copy-start(f32[512,128]{1,0:T(8,128)} %param.5) | copy-start | bytes 786436
where the time goes:
time: 218 us
  Pallas kernels  213 us (98%)
  local copies, waits for them, and re-layouts  4.35 us (2%)
    pallas_call x1, Pallas kernels, child(): pl.pallas_call(child_kernel, out_shape=(jax.ShapeDtypeStruct((P_SIZE, HB)...  123 us
    pallas_call x1, Pallas kernels, parent(): pl.pallas_call(parent_kernel, out_shape=(jax.ShapeDtypeStruct((PP, HB), F...  89.9 us

commit v1 on v0

v1 whole, which is shorter than its diff:
```python
import jax
import jax.numpy as jnp
from jax import lax
from jax.experimental import pallas as pl
from jax.experimental.pallas import tpu as pltpu
from jax.sharding import PartitionSpec as P

BS = 256
P_SIZE = 512
NP = 4096
PP = 512
HB = 128
NZ, NY = 8, 4
NH = NZ * NY
LO = 32
F32 = jnp.float32
HI = lax.Precision.HIGHEST
VMEM = pl.BlockSpec(memory_space=pltpu.VMEM)
SMEM = pl.BlockSpec(memory_space=pltpu.SMEM)
ANY = pl.BlockSpec(memory_space=pl.ANY)


def dot(a, b, dims):
    return lax.dot_general(a, b, (dims, ((), ())), precision=HI, preferred_element_type=F32)


def lane(x, i):
    return jnp.broadcast_to(x[:, i : i + 1], (8, 128))


def sub(x, i):
    return jnp.broadcast_to(x[i : i + 1, :], (8, x.shape[1]))


def chol_inv_128(tiles, hook=None):
    row = lax.broadcasted_iota(jnp.int32, (8, 128), 0)
    col = lax.broadcasted_iota(jnp.int32, (8, 128), 1)
    D = list(tiles)
    E = [jnp.where(col == row + 8 * q, 1.0, 0.0).astype(F32) for q in range(16)]
    for p in range(16):
        if hook is not None:
            hook(p)
        a, e = D[p], E[p]
        C = [lane(a, 8 * p + k) for k in range(8)]
        for k in range(8):
            rs = lax.rsqrt(sub(C[k], k))
            l = C[k] * rs
            lm = jnp.where(row > k, l, 0.0)
            for j in range(k + 1, 8):
                C[j] = C[j] - l * sub(l, j)
            ra = sub(a, k) * rs
            re = sub(e, k) * rs
            a = jnp.where(row == k, ra, a - lm * ra)
            e = jnp.where(row == k, re, e - lm * re)
        E[p] = e
        if p < 15:
            at = a.T
            for q in range(p + 1, 16):
                t, u = D[q], E[q]
                for k in range(8):
                    m = jnp.broadcast_to(at[8 * q : 8 * q + 8, k : k + 1], (8, 128))
                    t = t - m * sub(a, k)
                    u = u - m * sub(e, k)
                D[q], E[q] = t, u
    return E


def chol_inverse(rows, s_ref, m_ref, hooks=None):
    m_ref[...] = jnp.zeros((512, 512), F32)
    for b in range(4):
        o = 128 * b
        blk = slice(o, o + 128)
        A = rows(b)
        if b:
            A = A - dot(s_ref[:o, blk], s_ref[:o, o:], ((0,), (0,)))
        tiles = [A[8 * q : 8 * q + 8, :128] for q in range(16)]
        s_ref[blk, o:] = A
        W = jnp.concatenate(chol_inv_128(tiles, None if hooks is None else hooks(b)), axis=0)
        m_ref[blk, blk] = W
        if b < 3:
            s_ref[blk, o + 128 :] = dot(W, s_ref[blk, o + 128 :], ((1,), (0,)))
        if b:
            m_ref[blk, :o] = -dot(W, dot(s_ref[:o, blk], m_ref[:o, :o], ((0,), (0,))), ((1,), (0,)))


def chol_inverse_loop(rows, s_ref, m_ref, hook):
    m_ref[...] = jnp.zeros((512, 512), F32)
    s_ref[...] = jnp.zeros((512, 512), F32)

    @pl.loop(0, 4)
    def _(b):
        hook(b)
        o = pl.multiple_of(128 * b, 128)
        blk = pl.ds(o, 128)
        lead = s_ref[:, blk]
        A = rows(b) - dot(lead, s_ref[...], ((0,), (0,)))
        s_ref[blk, :] = A
        tiles = [s_ref[pl.ds(o + 8 * q, 8), blk] for q in range(16)]
        W = jnp.concatenate(chol_inv_128(tiles), axis=0)
        m_ref[blk, :] = -dot(W, dot(lead, m_ref[...], ((0,), (0,))), ((1,), (0,)))
        m_ref[blk, blk] = W
        s_ref[blk, :] = dot(W, A, ((1,), (0,)))


def child_phase(
    map_ref, front_hbm, g_ref, t_ref,
    front_ref, tt_ref, send_ref, all_ref, recv_ref, s_ref, m_ref, p_ref, tab_ref,
    s0y, r0y, s0z, r0z, s1z, r1z, s1y, r1y, s1f, r1f, sf, rf, loc, first_rows_done,
):
    me = lax.axis_index("col")
    br = lax.axis_index("branch")
    z, y = me // NY, lax.rem(me, NY)
    d = -1

    top = pltpu.make_async_copy(
        front_hbm.at[pl.ds(0, 4)], front_ref.at[pl.ds(0, 4)], loc.at[0]
    )
    top.start()
    rest = pltpu.make_async_copy(
        front_hbm.at[pl.ds(4, NH - 4)], front_ref.at[pl.ds(4, NH - 4)], loc.at[1]
    )
    rest.start()

    def at(zz, yy):
        return lax.rem(zz + 2 * NZ, NZ) * NY + lax.rem(yy + NY, NY)

    barrier = pltpu.get_barrier_semaphore()

    @pl.loop(1, NH)
    def _(k):
        pl.semaphore_signal(barrier, inc=1, device_id={"col": lax.rem(me + k, NH)})

    @pl.loop(1, 8)
    def _(k):
        pl.semaphore_signal(barrier, inc=1, device_id={"branch": lax.rem(br + k, 8)})

    for b in range(NP // BS):
        at_u = jnp.int32(-1)
        for u in range(14):
            at_u = jnp.where(map_ref[0, u] == b, u, at_u)
        keep = (at_u >= 0).astype(jnp.int32)
        src = jnp.where(at_u >= 0, 2 * at_u + 4, 0)
        for part in range(2):
            tab_ref[0, 2 * b + part] = src + part
            tab_ref[1, 2 * b + part] = keep

    top.wait()
    for k in range(4):
        tt_ref[:, 128 * k : 128 * k + 128] = front_ref[k].T

    pl.semaphore_wait(barrier, NH - 1 + 7)

    def copy(src, dst, ss, rs, to):
        return pltpu.make_async_remote_copy(
            src_ref=src, dst_ref=dst, send_sem=ss, recv_sem=rs, device_id={"col": to}
        )

    lo, hi = pl.ds(0, LO), pl.ds(LO, HB - LO)
    mid = (HB - LO) // 2
    half = (pl.ds(LO, mid), pl.ds(LO + mid, mid))
    own = pltpu.make_async_copy(tt_ref, all_ref.at[me], loc.at[2])
    own.start()

    order = [0, 1, -1, 2, -2, 3, -3, 4]
    fwd, bwd = [0, 1, 3, 5, 7], [0, 2, 4, 6]

    def behind(i):
        if isinstance(i, int):
            return order[i]
        return ((i + 1) // 2) * (2 * lax.rem(i, 2) - 1)

    def z1_send(chain, n, src=None):
        i, slot = chain[n], chain[n + 1]
        step = d if chain is fwd else -d
        blk = at(z - order[i] * d, y)
        src = all_ref.at[blk, hi] if src is None else src
        return copy(src, all_ref.at[blk, hi], s1z.at[slot - 1], r1z.at[slot - 1], at(z + step, y))

    def z1_recv(slot):
        ref = all_ref.at[at(z - order[slot] * d, y), hi]
        return copy(ref, ref, s1z.at[slot - 1], r1z.at[slot - 1], me)

    def y1(i, side, src=None):
        blk = at(z - behind(i) * d, y)
        src = all_ref.at[blk, hi] if src is None else src
        return copy(src, all_ref.at[blk, hi], s1y.at[i, side], r1y.at[i, side], at(z, y + 1 - 2 * side))

    def y1_recv(i, side):
        ref = all_ref.at[at(z - behind(i) * d, y - 1 + 2 * side), hi]
        return copy(ref, ref, s1y.at[i, side], r1y.at[i, side], me)

    def y1f(i, side):
        ref = all_ref.at[at(z - behind(i) * d, y - 1 + 2 * side), half[side]]
        return copy(ref, ref, s1f.at[i, side], r1f.at[i, side], at(z, y + 1 - 2 * side))

    def y1f_recv(i, side):
        ref = all_ref.at[at(z - behind(i) * d, y + 2), half[side]]
        return copy(ref, ref, s1f.at[i, side], r1f.at[i, side], me)

    def y0(k, src):
        return copy(src, all_ref.at[me, lo], s0y.at[k - 1], r0y.at[k - 1], at(z, y + k))

    def y0_recv(k):
        ref = all_ref.at[at(z, y - k), lo]
        return copy(ref, ref, s0y.at[k - 1], r0y.at[k - 1], me)

    def bundle(i):
        return all_ref.at[pl.ds(at(z - order[i] * d, 0), NY), lo]

    def z0_send(chain, n):
        i, slot = chain[n], chain[n + 1]
        step = d if chain is fwd else -d
        return copy(bundle(i), bundle(i), s0z.at[slot - 1], r0z.at[slot - 1], at(z + step, y))

    def z0_recv(slot):
        return copy(bundle(slot), bundle(slot), s0z.at[slot - 1], r0z.at[slot - 1], me)

    def fsend(k):
        to = lax.rem(me + k, NH)
        return copy(send_ref.at[to], recv_ref.at[me], sf.at[k - 1], rf.at[k - 1], to)

    def frecv(k):
        frm = lax.rem(me + NH - k, NH)
        return copy(send_ref.at[frm], recv_ref.at[frm], sf.at[k - 1], rf.at[k - 1], frm)

    def picked(h):
        return front_ref[tab_ref[0, h]].T * tab_ref[1, h].astype(F32)

    def prepare(first, last):
        @pl.loop(first, last)
        def _(k):
            h = lax.rem(me + k, NH)
            send_ref[h] = picked(h)

    def start_f(first, last):
        @pl.loop(first, last)
        def _(k):
            fsend(k).start()

    sends = []

    def go(c):
        c.start()
        sends.append(c)

    go(z1_send(fwd, 0, tt_ref.at[hi]))
    go(z1_send(bwd, 0, tt_ref.at[hi]))
    for k in (1, 3, 2):
        go(y0(k, tt_ref.at[lo]))
    for side in (0, 1):
        go(y1(0, side, tt_ref.at[hi]))
    rest.wait()
    prepare(1, 12)
    own.wait()
    for k in (1, 3, 2):
        y0_recv(k).wait_recv()
    go(z0_send(fwd, 0))
    go(z0_send(bwd, 0))
    for n in range(1, 5):
        for chain in (fwd, bwd):
            if n < len(chain):
                slot = chain[n]
                z1_recv(slot).wait_recv()
                if n + 1 < len(chain):
                    go(z1_send(chain, n))
                for side in (0, 1):
                    go(y1(slot, side))
        if n == 1:
            prepare(12, NH)
            recv_ref[me] = picked(me)
        for chain in (fwd, bwd):
            if n < len(chain):
                z0_recv(chain[n]).wait_recv()
                if n + 1 < len(chain):
                    go(z0_send(chain, n))
        start_f(1 + 4 * (n - 1), 1 + 4 * n)

    dist = lax.rem(z * d + NZ, NZ)
    i0 = jnp.where(dist <= 4, jnp.where(dist == 0, 0, 2 * dist - 1), 2 * (NZ - dist))
    for side in (0, 1):
        y1_recv(i0, side).wait_recv()
        y1f(i0, side).start()
    start_f(17, NH)
    for side in (0, 1):
        y1f_recv(i0, side).wait_recv()

    def forward(b):
        for n in range(2):
            i = 2 * b + n

            @pl.when(i != i0)
            def _():
                for side in (0, 1):
                    y1_recv(i, side).wait_recv()
                    y1f(i, side).start()

    chol_inverse_loop(lambda b: all_ref[b], s_ref, m_ref, forward)
    M = m_ref[...]
    g_ref[...] = dot(M, all_ref[me], ((1,), (1,)))

    @pl.loop(0, 8)
    def _(i):
        @pl.when(i != i0)
        def _():
            for side in (0, 1):
                y1f_recv(i, side).wait_recv()

    Y = dot(M, all_ref[tab_ref[0, me]], ((1,), (1,)))
    s_ref[:, :HB] = dot(M, Y, ((0,), (0,)))

    @pl.loop(0, NH // 4)
    def _(i):
        rows = all_ref[pl.ds(4 * i, 4)].reshape(4 * HB, P_SIZE)
        p_ref[pl.ds(4 * i, 4)] = dot(rows, s_ref[:, :HB], ((1,), (0,))).reshape(4, HB, HB)

    @pl.loop(1, NH)
    def _(k):
        frecv(k).wait_recv()

    keep_me = tab_ref[1, me].astype(F32)

    def strip(first, last):
        @pl.loop(first, last)
        def _(p):
            q = tab_ref[0, p]
            keep = tab_ref[1, p].astype(F32)
            t_ref[p] = keep * (recv_ref[q] - keep_me * p_ref[q])

    strip(0, 4)
    first_rows_done()
    strip(4, NH)

    def finish():
        for c in sends:
            c.wait_send()

        @pl.loop(0, 8)
        def _(i):
            for side in (0, 1):
                y1f(i, side).wait_send()

        @pl.loop(1, NH)
        def _(k):
            fsend(k).wait_send()

    return finish


PANEL = {(0, 1): 0, (0, 10): 1, (1, 7): 2, (2, 4): 3, (3, 1): 4}


def front_kernel(
    map_ref, front_hbm, pf_ref, g_ref, fac_ref, out_ref,
    front_ref, tt_ref, send_ref, all_ref, recv_ref, s_ref, m_ref, p_ref, t_ref, tab_ref,
    s0y, r0y, s0z, r0z, s1z, r1z, s1y, r1y, s1f, r1f, sf, rf, cloc,
    rtop, part, top, piv, pan, rx, sx, r2,
    s_rs, r_rs, s_pf, r_pf, s_ag, r_ag, s_x, r_x, s_2, r_2,
    s_vz, r_vz, s_vy, r_vy, s_vc, r_vc, s_nz, r_nz, s_ny, r_ny, loc,
):
    br, me = lax.axis_index("branch"), lax.axis_index("col")
    x, core = br // 2, lax.rem(br, 2)
    z, y = me // NY, lax.rem(me, NY)
    nb = 8

    def along_z(k):
        return lax.rem(z + k, NZ) * NY + y

    def along_y(k):
        return z * NY + lax.rem(y + k, NY)

    def copy(src, dst, ss, rs, **to):
        return pltpu.make_async_remote_copy(
            src_ref=src, dst_ref=dst, send_sem=ss, recv_sem=rs, device_id=to
        )

    def piece(b):
        return pl.ds(pl.multiple_of(16 * b, 16), 16)

    def rs_send(k):
        to = lax.rem(br + k, nb)
        return copy(t_ref.at[pl.ds(0, 4), piece(to)], rtop.at[br], s_rs.at[k - 1], r_rs.at[k - 1], branch=to)

    def rs_recv(k):
        frm = lax.rem(br + nb - k, nb)
        return copy(rtop.at[frm], rtop.at[frm], s_rs.at[k - 1], r_rs.at[k - 1], branch=frm)

    def pf_send(k):
        return copy(pf_ref.at[:, piece(k)], rtop.at[nb], s_pf.at[k - 1], r_pf, branch=jnp.int32(k))

    def start_rows():
        for k in range(1, nb):
            rs_send(k).start()

    finish_child = child_phase(
        map_ref, front_hbm, g_ref, t_ref,
        front_ref, tt_ref, send_ref, all_ref, recv_ref, s_ref, m_ref, p_ref, tab_ref,
        s0y, r0y, s0z, r0z, s1z, r1z, s1y, r1y, s1f, r1f, sf, rf, cloc, start_rows,
    )

    @pl.when(br == 0)
    def _():
        for k in range(1, nb):
            pf_send(k).start()

    def x_send(i):
        grp = 2 * i + 1 - core
        return copy(t_ref.at[pl.ds(4 * grp, 4)], rx.at[i], s_x.at[i], r_x.at[i], branch=br + 1 - 2 * core)

    for i in range(4):
        x_send(i).start()

    own = t_ref[0:4, piece(br), :]
    for k in range(1, nb):
        rs_recv(k).wait_recv()
        own = own + rtop[lax.rem(br + nb - k, nb)]
    part[...] = own

    @pl.when(br == 0)
    def _():
        part[...] += pf_ref[:, 0:16, :]

    @pl.when(br != 0)
    def _():
        copy(rtop.at[nb], rtop.at[nb], s_pf.at[0], r_pf, branch=jnp.int32(0)).wait_recv()
        part[...] += rtop[nb]

    def ag_send(k):
        to = lax.rem(br + k, nb)
        return copy(part, top.at[:, piece(br)], s_ag.at[k - 1], r_ag.at[k - 1], branch=to)

    def ag_recv(k):
        ref = top.at[:, piece(lax.rem(br + nb - k, nb))]
        return copy(part, ref, s_ag.at[k - 1], r_ag.at[k - 1], branch=br)

    for k in range(1, nb):
        ag_send(k).start()
    top[:, piece(br), :] = part[...]
    for k in range(1, nb):
        ag_recv(k).wait_recv()

    def chain(dist):
        step = jnp.where(dist <= 4, 1, NZ - 1)
        return step, jnp.logical_and(dist != 0, jnp.logical_and(dist != 4, dist != 5))

    ndist = lax.rem(z + NZ - br, NZ)
    nstep, nmore = chain(ndist)
    nhops = jnp.minimum(ndist, NZ - ndist)
    hrows = pl.ds(pl.multiple_of(64 * core, 64), 64)
    orows = pl.ds(pl.multiple_of(64 - 64 * core, 64), 64)
    other = br + 1 - 2 * core

    def vz(b, k):
        return copy(top.at[b, hrows], piv.at[y, b, hrows], s_vz.at[b, k - 1], r_vz.at[b], col=along_z(k))

    def vy(b, k):
        ref = piv.at[y, b, hrows]
        return copy(ref, ref, s_vy.at[b, k - 1], r_vy.at[b, k - 1], col=along_y(k))

    def vy_recv(b, k):
        ref = piv.at[lax.rem(y + NY - k, NY), b, hrows]
        return copy(ref, ref, s_vy.at[b, k - 1], r_vy.at[b, k - 1], col=me)

    def vc(b):
        ref = piv.at[:, b, hrows]
        return copy(ref, ref, s_vc.at[b], r_vc.at[b], branch=other)

    def vc_recv(b):
        ref = piv.at[:, b, orows]
        return copy(ref, ref, s_vc.at[b], r_vc.at[b], branch=other)

    def ny(k):
        return copy(pan.at[y], pan.at[y], s_ny.at[k - 1], r_ny.at[k - 1], col=along_y(k))

    def ny_recv(k):
        ref = pan.at[lax.rem(y + NY - k, NY)]
        return copy(ref, ref, s_ny.at[k - 1], r_ny.at[k - 1], col=me)

    lpiv = pltpu.make_async_copy(top.at[:, hrows], piv.at[y, :, hrows], loc.at[0])
    lpan = pltpu.make_async_copy(top, pan.at[y], loc.at[1])

    @pl.when(z == 0)
    def _():
        lpiv.start()
        for b in range(4):
            for k in (4, 5, 3, 6, 2, 7, 1):
                vz(b, k).start()
        lpiv.wait()

    @pl.when(z == br)
    def _():
        lpan.start()
        copy(top, pan.at[y], s_nz.at[0], r_nz, col=along_z(1)).start()
        copy(top, pan.at[y], s_nz.at[1], r_nz, col=along_z(7)).start()
        lpan.wait()

    def spread(b):
        @pl.when(z != 0)
        def _():
            ref = piv.at[y, b, hrows]
            copy(ref, ref, s_vz.at[b, 0], r_vz.at[b], col=me).wait_recv()

        for k in (2, 1, 3):
            vy(b, k).start()

    def panel_step(hops):
        @pl.when(nhops == hops)
        def _():
            if hops:
                copy(top, pan.at[y], s_nz.at[0], r_nz, col=me).wait_recv()

            @pl.when(nmore)
            def _():
                copy(pan.at[y], pan.at[y], s_nz.at[0], r_nz, col=along_z(nstep)).start()

            for k in (2, 1, 3):
                ny(k).start()

    def exchange(b):
        for k in (1, 3, 2):
            vy_recv(b, k).wait_recv()
        vc(b).start()

    def rows(b):
        vc_recv(b).wait_recv()
        return jnp.concatenate([piv[j, b] for j in range(b, 4)], axis=1)

    def x_recv(i):
        return copy(rx.at[i], rx.at[i], s_x.at[i], r_x.at[i], branch=br)

    def send2(k):
        to = lax.rem(x + k, 4)
        return copy(sx.at[to], r2.at[k - 1], s_2.at[k - 1], r_2.at[k - 1], branch=2 * to + core)

    def hooks(b):
        def hook(p):
            if p == 7 and b < 3:
                spread(b + 1)
            if p == 12 and b < 3:
                exchange(b + 1)
            if b == 0 and p == 6:
                for i in range(4):
                    x_recv(i).wait_recv()

                @pl.loop(0, 4)
                def _(i):
                    sx[i] = rx[i] + t_ref[pl.ds(4 * (2 * i + core), 4)]

            if b == 0 and p == 9:
                for k in (2, 1, 3):
                    send2(k).start()
            if (b, p) in PANEL:
                panel_step(PANEL[b, p])

        return hook

    spread(0)
    exchange(0)
    chol_inverse(rows, s_ref, m_ref, hooks)
    M = m_ref[...]
    F = dot(M, top[...].reshape(PP, HB), ((1,), (0,)))
    fac_ref[...] = F
    Z = dot(M, F, ((0,), (0,)))
    for k in range(1, 4):
        send2(k).wait_recv()
    for k in (1, 3, 2):
        ny_recv(k).wait_recv()

    s_ref[:, :HB] = Z

    @pl.loop(0, 4)
    def _(j):
        asm = pf_ref[j] + sx[x, j] + r2[0, j] + r2[1, j] + r2[2, j]
        rowsj = pan[j].reshape(PP, HB)
        out_ref[j] = asm - dot(rowsj, s_ref[:, :HB], ((0,), (0,)))

    for k in range(1, nb):
        rs_send(k).wait_send()
        ag_send(k).wait_send()

    @pl.when(br == 0)
    def _():
        for k in range(1, nb):
            pf_send(k).wait_send()

    for i in range(4):
        x_send(i).wait_send()
    for k in range(1, 4):
        send2(k).wait_send()
        ny(k).wait_send()
        for b in range(4):
            vy(b, k).wait_send()

    @pl.when(z == 0)
    def _():
        for b in range(4):
            for k in range(1, NZ):
                vz(b, k).wait_send()

    for b in range(4):
        vc(b).wait_send()

    @pl.when(jnp.logical_or(ndist == 0, nmore))
    def _():
        copy(top, pan.at[y], s_nz.at[0], r_nz, col=along_z(nstep)).wait_send()

    @pl.when(ndist == 0)
    def _():
        copy(top, pan.at[y], s_nz.at[1], r_nz, col=along_z(7)).wait_send()

    finish_child()


def fronts(extend_map, front, parent_front):
    dma = pltpu.SemaphoreType.DMA
    return pl.pallas_call(
        front_kernel,
        out_shape=(
            jax.ShapeDtypeStruct((P_SIZE, HB), F32),
            jax.ShapeDtypeStruct((PP, HB), F32),
            jax.ShapeDtypeStruct((4, HB, HB), F32),
        ),
        in_specs=[SMEM, ANY, VMEM],
        out_specs=(VMEM, VMEM, VMEM),
        scratch_shapes=[
            pltpu.VMEM((NH, HB, HB), F32),
            pltpu.VMEM((HB, P_SIZE), F32),
            pltpu.VMEM((NH, HB, HB), F32),
            pltpu.VMEM((NH, HB, P_SIZE), F32),
            pltpu.VMEM((NH, HB, HB), F32),
            pltpu.VMEM((P_SIZE, P_SIZE), F32),
            pltpu.VMEM((P_SIZE, P_SIZE), F32),
            pltpu.VMEM((NH, HB, HB), F32),
            pltpu.VMEM((NH, HB, HB), F32),
            pltpu.SMEM((2, NH), jnp.int32),
            dma((3,)), dma((3,)), dma((7,)), dma((7,)), dma((7,)), dma((7,)),
            dma((8, 2)), dma((8, 2)), dma((8, 2)), dma((8, 2)),
            dma((31,)), dma((31,)), dma((3,)),
            pltpu.VMEM((9, 4, 16, HB), F32),
            pltpu.VMEM((4, 16, HB), F32),
            pltpu.VMEM((4, HB, HB), F32),
            pltpu.VMEM((4, 4, HB, HB), F32),
            pltpu.VMEM((4, 4, HB, HB), F32),
            pltpu.VMEM((4, 4, HB, HB), F32),
            pltpu.VMEM((4, 4, HB, HB), F32),
            pltpu.VMEM((3, 4, HB, HB), F32),
            dma((7,)), dma((7,)), dma((7,)), dma(()), dma((7,)), dma((7,)),
            dma((4,)), dma((4,)), dma((3,)), dma((3,)),
            dma((4, 7)), dma((4,)), dma((4, 3)), dma((4, 3)), dma((4,)), dma((4,)),
            dma((2,)), dma(()), dma((3,)), dma((3,)), dma((2,)),
        ],
        compiler_params=pltpu.CompilerParams(
            collective_id=0, has_side_effects=True, vmem_limit_bytes=56 << 20
        ),
        name="fronts",
    )(extend_map, front, parent_front)


def on_device(child_fronts, extend_map, parent_front):
    front = child_fronts[0]
    child_mine, parent_mine, result = fronts(
        extend_map, front.reshape(NH, HB, HB), parent_front.reshape(4, HB, HB)
    )
    return (child_mine[None], parent_mine, result.reshape(parent_front.shape))


def solution(mesh):
    in_specs = (P("branch", None, "col"), P("branch", None), P("branch", "col"))
    out_specs = (P("branch", None, "col"), P(None, "col"), P("branch", "col"))
    return jax.shard_map(
        on_device, mesh=mesh, in_specs=in_specs, out_specs=out_specs, check_vma=False
    )
```

time: 218 us -> 189 us (0.87)
  the two profiles are of different devices: /device:TPU:160 before, /device:TPU:33 now
where the time goes in v1:
time: 189 us
  Pallas kernels  183 us (97%)
  local copies, waits for them, and re-layouts  5.01 us (3%)
    pallas_call x1, Pallas kernels, fronts(): pl.pallas_call(front_kernel, out_shape=(jax.ShapeDtypeStruct((P_SIZE, HB)...  183 us
    unnamed x3, local copies, waits for them, and re-layouts  5.01 us

profile of v1, /device:TPU:33, one launch (start us, length us, event | category | flops | bytes accessed | tf_op | source)
XLA Modules:
  0.0 188.6 jit_solution(4566749617494949028)
XLA Ops:
  0.6 182.9 %fronts.1 = (f32[512,128]{1,0:T(8,128)}, f32[512,128]{1,0:T(8,128)}, f32[4,128,128]{2,1,0:T(8,128)}) custom-call(s32[1,14]{1,0:T(1,128)} %map_ref.1, f32[32,128,128]{2,1,0:T(8,128)} %bitcast.4, f32[4,128,128]{2,1,0:T(8,128)} %bitcast.5), custom_call_target="tpu_custom_call" | custom-call | tf_op jit(solution)/shard_map/fronts/pallas_call | solution.py:615
  183.5 1.7 copy.9
  185.2 1.7 copy.10
  186.9 1.7 copy.11

commit v2 on v1

--- a/solution.py
+++ b/solution.py
@@ -17,7 +17,7 @@
 HI = lax.Precision.HIGHEST
 VMEM = pl.BlockSpec(memory_space=pltpu.VMEM)
 SMEM = pl.BlockSpec(memory_space=pltpu.SMEM)
-ANY = pl.BlockSpec(memory_space=pl.ANY)
+HBM = pl.BlockSpec(memory_space=pltpu.HBM)
 
 
 def dot(a, b, dims):
@@ -233,9 +233,11 @@
             send_ref[h] = picked(h)
 
     def start_f(first, last):
-        @pl.loop(first, last)
-        def _(k):
-            fsend(k).start()
+        @pl.when(z != 0)
+        def _():
+            @pl.loop(first, last)
+            def _(k):
+                fsend(k).start()
 
     sends = []
 
@@ -315,7 +317,9 @@
 
     @pl.loop(1, NH)
     def _(k):
-        frecv(k).wait_recv()
+        @pl.when(lax.rem(me + NH - k, NH) >= NY)
+        def _():
+            frecv(k).wait_recv()
 
     keep_me = tab_ref[1, me].astype(F32)
 
@@ -339,14 +343,16 @@
             for side in (0, 1):
                 y1f(i, side).wait_send()
 
-        @pl.loop(1, NH)
-        def _(k):
-            fsend(k).wait_send()
+        @pl.when(z != 0)
+        def _():
+            @pl.loop(1, NH)
+            def _(k):
+                fsend(k).wait_send()
 
     return finish
 
 
-PANEL = {(0, 1): 0, (0, 10): 1, (1, 7): 2, (2, 4): 3, (3, 1): 4}
+SLOTS = {(0, 2): 0, (0, 9): 1, (1, 0): 2, (1, 7): 3, (1, 14): 4, (2, 5): 5, (2, 12): 6, (3, 3): 7}
 
 
 def front_kernel(
@@ -468,12 +474,15 @@
         ref = piv.at[:, b, orows]
         return copy(ref, ref, s_vc.at[b], r_vc.at[b], branch=other)
 
-    def ny(k):
-        return copy(pan.at[y], pan.at[y], s_ny.at[k - 1], r_ny.at[k - 1], col=along_y(k))
-
-    def ny_recv(k):
-        ref = pan.at[lax.rem(y + NY - k, NY)]
-        return copy(ref, ref, s_ny.at[k - 1], r_ny.at[k - 1], col=me)
+    def nz(q, side, src, to):
+        return copy(src, pan.at[y, q], s_nz.at[q, side], r_nz.at[q], col=to)
+
+    def ny(q, k):
+        return copy(pan.at[y, q], pan.at[y, q], s_ny.at[q, k - 1], r_ny.at[q, k - 1], col=along_y(k))
+
+    def ny_recv(q, k):
+        ref = pan.at[lax.rem(y + NY - k, NY), q]
+        return copy(ref, ref, s_ny.at[q, k - 1], r_ny.at[q, k - 1], col=me)
 
     lpiv = pltpu.make_async_copy(top.at[:, hrows], piv.at[y, :, hrows], loc.at[0])
     lpan = pltpu.make_async_copy(top, pan.at[y], loc.at[1])
@@ -489,8 +498,9 @@
     @pl.when(z == br)
     def _():
         lpan.start()
-        copy(top, pan.at[y], s_nz.at[0], r_nz, col=along_z(1)).start()
-        copy(top, pan.at[y], s_nz.at[1], r_nz, col=along_z(7)).start()
+        for q in range(4):
+            nz(q, 0, top.at[q], along_z(1)).start()
+            nz(q, 1, top.at[q], along_z(7)).start()
         lpan.wait()
 
     def spread(b):
@@ -502,18 +512,21 @@
         for k in (2, 1, 3):
             vy(b, k).start()
 
-    def panel_step(hops):
-        @pl.when(nhops == hops)
-        def _():
-            if hops:
-                copy(top, pan.at[y], s_nz.at[0], r_nz, col=me).wait_recv()
+    def panel_step(slot):
+        q = slot - nhops
+
+        @pl.when(jnp.logical_and(q >= 0, q < 4))
+        def _():
+            @pl.when(nhops != 0)
+            def _():
+                nz(q, 0, pan.at[y, q], me).wait_recv()
 
             @pl.when(nmore)
             def _():
-                copy(pan.at[y], pan.at[y], s_nz.at[0], r_nz, col=along_z(nstep)).start()
+                nz(q, 0, pan.at[y, q], along_z(nstep)).start()
 
             for k in (2, 1, 3):
-                ny(k).start()
+                ny(q, k).start()
 
     def exchange(b):
         for k in (1, 3, 2):
@@ -548,8 +561,8 @@
             if b == 0 and p == 9:
                 for k in (2, 1, 3):
                     send2(k).start()
-            if (b, p) in PANEL:
-                panel_step(PANEL[b, p])
+            if (b, p) in SLOTS:
+                panel_step(SLOTS[b, p])
 
         return hook
 
@@ -562,8 +575,9 @@
     Z = dot(M, F, ((0,), (0,)))
     for k in range(1, 4):
         send2(k).wait_recv()
-    for k in (1, 3, 2):
-        ny_recv(k).wait_recv()
+    for q in range(4):
+        for k in (1, 3, 2):
+            ny_recv(q, k).wait_recv()
 
     s_ref[:, :HB] = Z
 
@@ -586,9 +600,9 @@
         x_send(i).wait_send()
     for k in range(1, 4):
         send2(k).wait_send()
-        ny(k).wait_send()
         for b in range(4):
             vy(b, k).wait_send()
+            ny(b, k).wait_send()
 
     @pl.when(z == 0)
     def _():
@@ -599,13 +613,14 @@
     for b in range(4):
         vc(b).wait_send()
 
-    @pl.when(jnp.logical_or(ndist == 0, nmore))
-    def _():
-        copy(top, pan.at[y], s_nz.at[0], r_nz, col=along_z(nstep)).wait_send()
-
-    @pl.when(ndist == 0)
-    def _():
-        copy(top, pan.at[y], s_nz.at[1], r_nz, col=along_z(7)).wait_send()
+    for q in range(4):
+        @pl.when(jnp.logical_or(ndist == 0, nmore))
+        def _():
+            nz(q, 0, pan.at[y, q], along_z(nstep)).wait_send()
+
+        @pl.when(ndist == 0)
+        def _():
+            nz(q, 1, pan.at[y, q], along_z(7)).wait_send()
 
     finish_child()
 
@@ -619,7 +634,7 @@
             jax.ShapeDtypeStruct((PP, HB), F32),
             jax.ShapeDtypeStruct((4, HB, HB), F32),
         ),
-        in_specs=[SMEM, ANY, VMEM],
+        in_specs=[SMEM, HBM, VMEM],
         out_specs=(VMEM, VMEM, VMEM),
         scratch_shapes=[
             pltpu.VMEM((NH, HB, HB), F32),
@@ -646,10 +661,10 @@
             dma((7,)), dma((7,)), dma((7,)), dma(()), dma((7,)), dma((7,)),
             dma((4,)), dma((4,)), dma((3,)), dma((3,)),
             dma((4, 7)), dma((4,)), dma((4, 3)), dma((4, 3)), dma((4,)), dma((4,)),
-            dma((2,)), dma(()), dma((3,)), dma((3,)), dma((2,)),
+            dma((4, 2)), dma((4,)), dma((4, 3)), dma((4, 3)), dma((2,)),
         ],
         compiler_params=pltpu.CompilerParams(
-            collective_id=0, has_side_effects=True, vmem_limit_bytes=56 << 20
+            collective_id=0, has_side_effects=True, vmem_limit_bytes=40 << 20
         ),
         name="fronts",
     )(extend_map, front, parent_front)

time: 189 us -> 186 us (0.984)
  Pallas kernels: 183 us -> 180 us
    pallas_call x1, Pallas kernels: 183 us -> 180 us  [fronts(): pl.pallas_call(front_kernel, out_shape=(jax.ShapeDtypeStruct((P_SIZE, HB)...]
    unnamed x3 -> x9, local copies, waits for them, and re-layouts: 5.01 us -> 5.3 us
where the time goes in v2:
time: 186 us
  Pallas kernels  180 us (97%)
  local copies, waits for them, and re-layouts  5.3 us (3%)
    pallas_call x1, Pallas kernels, fronts(): pl.pallas_call(front_kernel, out_shape=(jax.ShapeDtypeStruct((P_SIZE, HB)...  180 us
    unnamed x9, local copies, waits for them, and re-layouts  5.3 us

profile of v2, /device:TPU:33, one launch (start us, length us, event | category | flops | bytes accessed | tf_op | source)
XLA Modules:
  0.0 186.3 jit_solution(14740591324721584680)
XLA Ops:
  0.6 0.0 copy-start
  0.6 1.6 copy-done
  2.2 0.0 copy-start.1
  2.2 0.9 copy-done.1
  3.2 0.0 copy-start.2
  3.2 0.7 copy-done.2
  3.8 180.4 %fronts.1 = (f32[512,128]{1,0:T(8,128)S(1)}, f32[512,128]{1,0:T(8,128)S(1)}, f32[4,128,128]{2,1,0:T(8,128)S(1)}) custom-call(s32[1,14]{1,0:T(1,128)S(1)} %copy-done.2, f32[32,128,128]{2,1,0:T(8,128)S(1)} %bitcast.4, f32[4,128,128]{2,1,0:T(8,128)S(1)} %bitcast.5), custom_call_target="tpu_custom_call" | custom-call | tf_op jit(solution)/shard_map/fronts/pallas_call | solution.py:630
  184.2 0.7 copy.9
  184.9 0.7 copy.10
  185.6 0.7 copy.11
Async XLA Ops:
  0.6 1.6 copy-start
  2.2 0.9 copy-start.1
  3.2 0.7 copy-start.2

commit v3 on v2

--- a/solution.py
+++ b/solution.py
@@ -12,7 +12,7 @@
 HB = 128
 NZ, NY = 8, 4
 NH = NZ * NY
-LO = 32
+LO = 48
 F32 = jnp.float32
 HI = lax.Precision.HIGHEST
 VMEM = pl.BlockSpec(memory_space=pltpu.VMEM)

time: 186 us -> 197 us (1.059)
  Pallas kernels: 180 us -> 191 us
    pallas_call x1, Pallas kernels: 180 us -> 191 us  [fronts(): pl.pallas_call(front_kernel, out_shape=(jax.ShapeDtypeStruct((P_SIZE, HB)...]
where the time goes in v3:
time: 197 us
  Pallas kernels  191 us (97%)
  local copies, waits for them, and re-layouts  5.3 us (3%)
    pallas_call x1, Pallas kernels, fronts(): pl.pallas_call(front_kernel, out_shape=(jax.ShapeDtypeStruct((P_SIZE, HB)...  191 us
    unnamed x9, local copies, waits for them, and re-layouts  5.3 us

profile of v3, /device:TPU:33, one launch (start us, length us, event | category | flops | bytes accessed | tf_op | source)
XLA Modules:
  0.0 197.1 jit_solution(10525243676390890733)
XLA Ops:
  0.6 0.0 copy-start
  0.6 1.6 copy-done
  2.2 0.0 copy-start.1
  2.2 0.9 copy-done.1
  3.2 0.0 copy-start.2
  3.2 0.7 copy-done.2
  3.8 191.2 %fronts.1 = (f32[512,128]{1,0:T(8,128)S(1)}, f32[512,128]{1,0:T(8,128)S(1)}, f32[4,128,128]{2,1,0:T(8,128)S(1)}) custom-call(s32[1,14]{1,0:T(1,128)S(1)} %copy-done.2, f32[32,128,128]{2,1,0:T(8,128)S(1)} %bitcast.4, f32[4,128,128]{2,1,0:T(8,128)S(1)} %bitcast.5), custom_call_target="tpu_custom_call" | custom-call | tf_op jit(solution)/shard_map/fronts/pallas_call | solution.py:630
  195.0 0.7 copy.9
  195.7 0.7 copy.10
  196.4 0.7 copy.11
Async XLA Ops:
  0.6 1.6 copy-start
  2.2 0.9 copy-start.1
  3.2 0.7 copy-start.2
